TPU v7x, 32 devices: a whole 2x2x4 slice. The times are simulated.
32 devices in a mesh: section: 2 (over x), patch: 4 (over z), fsdp: 4 (over y, core).
Axes of the slice: x: 2, y: 2, z: 4, core: 2. Of those that a mesh axis runs over, the one named last changes fastest.
Arguments:
- latent: float32 [8, 4, 256, 64], P('fsdp', 'patch', 'section'), may hold values from -60 to 60
- counts: int32 [8, 4], P('fsdp'), may hold values from 64 to 256, as said below
- steps_idx: int32 [8], P('fsdp'), may hold values from 0 to 49
- embed_weight: bfloat16 [64, 1536], replicated, may hold values from -0.75 to 0.75
- wqkv: bfloat16 [2, 1536, 4608], P('section', 'fsdp'), may hold values from -0.15625 to 0.15625
- wo: bfloat16 [2, 1536, 1536], P('section', 'fsdp'), may hold values from -0.15625 to 0.15625
- qk_gain: float32 [2, 3072], P('section'), may hold values from 0.1 to 1.9
- modulation: float32 [2, 50, 4608], P('section'), may hold values from -3 to 3
- head_mod: float32 [50, 3072], replicated, may hold values from -3 to 3
- head_weight: bfloat16 [1536, 64], replicated, may hold values from -0.15625 to 0.15625
- stale_cache: bfloat16 [2, 8, 4, 256, 3072], P('section', 'fsdp', 'patch'), may hold values from -210 to 210
Outputs:
- velocity: float32 [8, 4, 256, 64], P('fsdp', 'patch', 'section')
- new_latent: float32 [8, 4, 256, 64], P('fsdp', 'patch', 'section')
- cache_out: bfloat16 [2, 8, 4, 256, 3072], P('section', 'fsdp', 'patch')
Inputs may be any that keep to these rules, and one draw needn't show every extreme that they name: `counts`: in every video one patch holds exactly 256 tokens.
All inputs are finite; a program needn't handle non-finite values.
Results may differ from a plain program's by a relative error of at most 0.0071.
Values may be sent and summed in bfloat16 or wider, within the bound.
A program may use at most 192 MiB of HBM per device.

v0:
```python
import math
import jax
import jax.numpy as jnp
from jax import lax
from jax.sharding import PartitionSpec as P

HEADS = 12
HD = 128
TSTEPS = 50
EPS = 1e-06


def shifted(shard, axis, by):
    devices = lax.axis_size(axis)
    pairs = [(i, i + by) for i in range(devices) if 0 <= i + by < devices]
    return lax.ppermute(shard, axis, pairs)


def layer_norm(hidden):
    center = hidden - jnp.mean(hidden, axis=-1, keepdims=True)
    return center * lax.rsqrt(jnp.mean(center * center, axis=-1, keepdims=True) + EPS)


def rms_norm(values_in, gain_vec):
    return (
        values_in
        * lax.rsqrt(jnp.mean(values_in * values_in, axis=-1, keepdims=True) + EPS)
        * gain_vec
    )


def sigma_of(step_float):
    remain = 1.0 - step_float / TSTEPS
    return 5.0 * remain / (1.0 + 4.0 * remain)


def dense_attend(queries, key_rows, value_rows, key_live):
    groups, query_count = (queries.shape[0], queries.shape[1])
    query_heads = queries.reshape(groups, query_count, HEADS, HD)
    key_heads = key_rows.reshape(groups, key_rows.shape[1], HEADS, HD)
    value_heads = value_rows.reshape(groups, value_rows.shape[1], HEADS, HD)
    scores = jnp.einsum(
        "gqhd,gkhd->ghqk", query_heads, key_heads, preferred_element_type=jnp.float32
    ) / math.sqrt(HD)
    scores = jnp.where(key_live[:, None, None, :], scores, -jnp.inf)
    top_score = jnp.max(scores, axis=-1, keepdims=True)
    exp_scores = jnp.exp(scores - top_score)
    denom_sum = jnp.sum(exp_scores, axis=-1)
    mixed_out = jnp.einsum(
        "ghqk,gkhd->gqhd",
        exp_scores.astype(jnp.bfloat16),
        value_heads,
        preferred_element_type=jnp.float32,
    )
    mixed_out = mixed_out / jnp.transpose(denom_sum, (0, 2, 1))[..., None]
    return mixed_out.reshape(groups, query_count, HEADS * HD).astype(jnp.bfloat16)


def run_layer(hidden, modulation_rows, project_in, project_out, gain_rows, attend_fn):
    groups, slot_count, model_width = hidden.shape
    shift_vec = modulation_rows[:, None, :model_width]
    scale_vec = modulation_rows[:, None, model_width : 2 * model_width]
    gate_vec = modulation_rows[:, None, 2 * model_width :]
    normed = (layer_norm(hidden) * (1.0 + scale_vec) + shift_vec).astype(jnp.bfloat16)
    projected = project_in(normed.reshape(-1, model_width))
    projected = projected.reshape(groups, slot_count, 3 * model_width)
    queries = rms_norm(projected[..., :model_width], gain_rows[:model_width]).astype(jnp.bfloat16)
    fresh_keys = rms_norm(
        projected[..., model_width : 2 * model_width], gain_rows[model_width:]
    ).astype(jnp.bfloat16)
    fresh_values = projected[..., 2 * model_width :].astype(jnp.bfloat16)
    fresh_kv = jnp.concatenate([fresh_keys, fresh_values], axis=-1)
    attended = attend_fn(queries, fresh_kv)
    update = project_out(attended.reshape(-1, model_width))
    return (hidden + gate_vec * update.reshape(groups, slot_count, model_width), fresh_kv)


def body(
    latent,
    counts,
    steps_idx,
    embed_weight,
    wqkv,
    wo,
    qk_gain,
    modulation,
    head_mod,
    head_weight,
    stale_cache,
):
    section_index = lax.axis_index("section")
    own_patch = lax.axis_index("patch")
    first_section = section_index == 0
    videos = latent.shape[0]
    patch_rows = stale_cache.shape[3]
    model_width = embed_weight.shape[1]
    patch_count = counts.shape[1]
    zero_index = jnp.zeros((), jnp.int32)
    proj_full, out_full = (
        lax.all_gather(wqkv, "fsdp", axis=1, tiled=True),
        lax.all_gather(wo, "fsdp", axis=1, tiled=True),
    )
    proj_full = proj_full[0]
    out_full = out_full[0]

    def project_in(left):
        return jnp.dot(left, proj_full, preferred_element_type=jnp.float32)

    def project_out(left):
        return jnp.dot(left, out_full, preferred_element_type=jnp.float32)

    rows_full = lax.all_gather(latent.astype(jnp.bfloat16), "section", axis=2, tiled=True)
    start_hidden = jnp.dot(
        rows_full.reshape(-1, rows_full.shape[3]), embed_weight, preferred_element_type=jnp.float32
    )
    start_hidden = start_hidden.reshape(videos, patch_rows, model_width)
    step_onehot = (jnp.arange(TSTEPS, dtype=jnp.int32)[None, :] == steps_idx[:, None]).astype(
        jnp.float32
    )
    modulation_all = jnp.dot(step_onehot, modulation[0], precision=lax.Precision.HIGHEST)
    head_rows = jnp.dot(step_onehot, head_mod, precision=lax.Precision.HIGHEST)
    gain_rows = qk_gain[0]
    slot_iota = jnp.arange(patch_rows, dtype=jnp.int32)
    own_count = jnp.sum(
        jnp.where(jnp.arange(patch_count, dtype=jnp.int32)[None, :] == own_patch, counts, 0), axis=1
    )
    own_live = slot_iota[None, :] < own_count[:, None]
    key_live_all = (slot_iota[None, None, :] < counts[:, :, None]).reshape(
        videos, patch_count * patch_rows
    )
    stale_all = lax.all_gather(stale_cache, "patch", axis=2, tiled=True)[0].reshape(
        videos, patch_count * patch_rows, 2 * model_width
    )
    group_size = videos // videos
    received = jnp.zeros((group_size, patch_rows, model_width), jnp.float32)
    hidden_end = jnp.zeros((videos, patch_rows, model_width), jnp.float32)
    cache_buf = jnp.zeros((videos, patch_rows, 2 * model_width), jnp.bfloat16)
    for tick_index in range(videos + 1):
        group_index = jnp.clip(
            jnp.where(first_section, tick_index, tick_index - 1), 0, videos - 1
        ).astype(jnp.int32)
        first_video = group_index * group_size
        source_group = min(tick_index, videos - 1)
        source_zero = start_hidden[source_group * group_size : (source_group + 1) * group_size]
        hidden_in = jnp.where(first_section, source_zero, received)
        modulation_group = lax.dynamic_slice_in_dim(modulation_all, first_video, group_size, 0)
        stale_group = lax.dynamic_slice_in_dim(stale_all, first_video, group_size, 0)
        live_group = lax.dynamic_slice_in_dim(key_live_all, first_video, group_size, 0)

        def attend_fn(queries, fresh_kv, stale_group=stale_group, live_group=live_group):
            seen_rows = lax.dynamic_update_slice(
                stale_group, fresh_kv, (zero_index, own_patch * patch_rows, zero_index)
            )
            return dense_attend(
                queries, seen_rows[..., :model_width], seen_rows[..., model_width:], live_group
            )

        hidden_out, fresh_kv = run_layer(
            hidden_in, modulation_group, project_in, project_out, gain_rows, attend_fn
        )
        own_group = lax.dynamic_slice_in_dim(own_live, first_video, group_size, 0)
        fresh_kv = jnp.where(own_group[..., None], fresh_kv, jnp.zeros_like(fresh_kv))
        is_valid = jnp.where(first_section, tick_index < videos, tick_index >= 1)
        cache_buf = jnp.where(
            is_valid,
            lax.dynamic_update_slice(cache_buf, fresh_kv, (first_video, zero_index, zero_index)),
            cache_buf,
        )
        hidden_end = jnp.where(
            is_valid,
            lax.dynamic_update_slice(hidden_end, hidden_out, (first_video, zero_index, zero_index)),
            hidden_end,
        )
        if tick_index < videos:
            received = shifted(hidden_out.astype(jnp.bfloat16), "section", 1).astype(jnp.float32)
    head_in = (
        layer_norm(hidden_end) * (1.0 + head_rows[:, None, model_width:])
        + head_rows[:, None, :model_width]
    ).astype(jnp.bfloat16)
    velocity = jnp.dot(
        head_in.reshape(-1, model_width), head_weight, preferred_element_type=jnp.float32
    )
    velocity = velocity.reshape(videos, patch_rows, head_weight.shape[1])
    velocity = jnp.where(own_live[..., None], velocity, jnp.zeros_like(velocity))
    half_rows = patch_rows // 2
    returned = shifted(velocity[:, :half_rows].astype(jnp.bfloat16), "section", -1).astype(
        jnp.float32
    )
    mine_half = jnp.where(first_section, returned, velocity[:, half_rows:])
    step_float = steps_idx.astype(jnp.float32)
    step_delta = sigma_of(step_float + 1.0) - sigma_of(step_float)
    new_latent = latent + step_delta[:, None, None, None] * mine_half[:, None]
    return (mine_half[:, None], new_latent, cache_buf[None, :, None])


def solution(mesh):
    in_specs = (
        P("fsdp", "patch", "section", None),
        P("fsdp", None),
        P("fsdp"),
        P(),
        P("section", "fsdp", None),
        P("section", "fsdp", None),
        P("section", None),
        P("section", None, None),
        P(),
        P(),
        P("section", "fsdp", "patch", None, None),
    )
    out_specs = (
        P("fsdp", "patch", "section", None),
        P("fsdp", "patch", "section", None),
        P("section", "fsdp", "patch", None, None),
    )
    return jax.shard_map(body, mesh=mesh, in_specs=in_specs, out_specs=out_specs, check_vma=False)
```

profile of v0, /device:TPU:0, one launch (start us, length us, event | category | flops | bytes accessed | tf_op | source)
XLA Modules:
  0.0 515.3 jit_solution(11341558818491198296)
XLA Ops:
  7.2 0.7 all-gather.4.cloned.1.call-update
  8.0 0.7 all-gather.6.cloned.1.call-update
  8.7 0.7 all-gather.8.cloned.1.call-update
  9.5 5.5 %all_gather.12 = bf16[2,1,256,64]{2,3,1,0:T(8,128)(2,1)S(1)} all-gather(bf16[2,1,128,64]{2,3,1,0:T(8,128)(2,1)S(1)} %convert_element_type.99), channel_id=1, replica_groups=mesh['section'=2,'patch'=4,'fsdp'=4] {'section'}, dimensions={2}, use_global_device_ids=true | all-gather | bytes 98304 | tf_op jit(solution)/shard_map/all_gather | solution.py:112
  15.1 0.6 fusion.136
  15.9 1.4 copy-done.1
  18.2 0.5 fusion.89
  18.8 211.8 %all-gather.4.cloned.1.call-done = bf16[1,2,4,256,3072]{4,3,2,1,0:T(8,128)(2,1)} async-done(((bf16[1,2,1,256,3072]{4,3,2,1,0:T(8,128)(2,1)}), bf16[1,2,4,256,3072]{4,3,2,1,0:T(8,128)(2,1)}) %all-gather.4.cloned.1.call-update) | async-done | bytes 12582928 | tf_op jit(solution)/shard_map/all_gather | solution.py:131
  230.6 16.0 %constant_dynamic-slice_fusion.3 = (bf16[1,1024,3072]{2,1,0:T(8,128)(2,1)}, bf16[1,1024,3072]{2,1,0:T(8,128)(2,1)}, bf16[1,1024,3072]{2,1,0:T(8,128)(2,1)}) fusion(bf16[2,1024,3072]{2,1,0:T(8,128)(2,1)} %bitcast.193, s32[]{:T(128)S(6)} %min.12, s32[]{:T(128)S(6)} %min.11, s32[]{:T(128)S(6)} %min.10), kind=kLoop, calls=%fused_computation.146 | loop fusion | bytes 37748748 | tf_op jit(solution)/shard_map/dynamic_slice | solution.py:147
  246.6 8.7 %copy.54 = bf16[1,1024,3072]{1,2,0:T(8,128)(2,1)} copy(bf16[1,1024,3072]{2,1,0:T(8,128)(2,1)} %get-tuple-element.34) | data formatting | bytes 12582912
  255.3 66.1 %all-gather.6.cloned.1.call-done = bf16[1,1536,4608]{2,1,0:T(8,128)(2,1)} async-done(((bf16[1,384,4608]{2,1,0:T(8,128)(2,1)}), bf16[1,1536,4608]{2,1,0:T(8,128)(2,1)}) %all-gather.6.cloned.1.call-update) | async-done | bytes 14155792 | tf_op jit(solution)/shard_map/all_gather | solution.py:100
  321.4 7.8 %fusion.15 = f32[1,256,4608]{2,1,0:T(8,128)S(1)} fusion(bf16[1,1536,4608]{2,1,0:T(8,128)(2,1)} %all-gather.6.cloned.1.call-done, f32[512,1536]{1,0:T(8,128)} %copy-done.1, f32[1536]{0:T(1024)S(1)} %get-tuple-element.23, f32[1536]{0:T(1024)S(1)} %get-tuple-element.19, f32[256]{0:T(256)S(1)} %add_rsqrt_fusion.9, f32[256]{0:T(256)S(1)} %broadcast_multiply_fusion.3, ...), kind=kOutput, calls=%fused_computation.21 | convolution fusion | flops 3626237952 | bytes 20461568 | tf_op jit(solution)/shard_map/dot_general | solution.py:107
  329.9 2.1 broadcast_in_dim.155
  332.0 1.8 select_dynamic-update-slice_fusion.1
  333.8 1.6 copy.29
  335.6 2.7 constant_dynamic-update-slice_fusion.3
  338.3 3.6 fusion.134
  341.9 2.0 fusion.6
  343.9 3.0 fusion.9
  347.0 3.3 fusion.80
  350.3 10.2 %all-gather.8.cloned.1.call-done = bf16[1,1536,1536]{2,1,0:T(8,128)(2,1)} async-done(((bf16[1,384,1536]{2,1,0:T(8,128)(2,1)}), bf16[1,1536,1536]{2,1,0:T(8,128)(2,1)}) %all-gather.8.cloned.1.call-update) | async-done | bytes 4718608 | tf_op jit(solution)/shard_map/all_gather | solution.py:101
  360.5 2.0 broadcast_in_dim.85
  362.5 1.0 copy-done.2
  363.5 4.9 bitcast_dynamic-update-slice_fusion.1
  368.4 3.4 collective-permute-start
  371.8 8.8 %copy.55 = bf16[1,1024,3072]{1,2,0:T(8,128)(2,1)} copy(bf16[1,1024,3072]{2,1,0:T(8,128)(2,1)} %get-tuple-element.33) | data formatting | bytes 12582912
  380.6 8.3 %collective-permute-done = bf16[1,256,1536]{2,1,0:T(8,128)(2,1)S(1)} collective-permute-done((bf16[1,256,1536]{2,1,0:T(8,128)(2,1)S(1)}, bf16[1,256,1536]{2,1,0:T(8,128)(2,1)S(1)}, u32[]{:S(2)}, u32[]{:S(2)}) %collective-permute-start) | collective-permute-done | bytes 786464 | tf_op jit(solution)/shard_map/ppermute | solution.py:16
  389.0 1.6 fusion.130
  390.6 1.8 multiply_reduce_fusion.6
  392.4 7.5 %fusion.18 = f32[1,256,4608]{2,1,0:T(8,128)S(1)} fusion(bf16[1,1536,4608]{2,1,0:T(8,128)(2,1)} %all-gather.6.cloned.1.call-done, f32[1536]{0:T(1024)S(1)} %get-tuple-element.22, f32[1536]{0:T(1024)S(1)} %get-tuple-element.17, f32[256]{0:T(256)S(1)} %add_rsqrt_fusion.6, f32[256]{0:T(256)S(1)} %broadcast_multiply_fusion.2, ...), kind=kOutput, calls=%fused_computation.22 | convolution fusion | flops 3626631168 | bytes 21252096 | tf_op jit(solution)/shard_map/dot_general | solution.py:107
  400.3 1.1 multiply_convert_fusion.2
  401.5 1.8 select_dynamic-update-slice_fusion
  403.3 1.6 copy.33
  404.9 2.7 constant_dynamic-update-slice_fusion.2
  407.6 6.3 %fusion.133 = (bf16[1,1024,1536]{1,2,0:T(8,128)(2,1)}, bf16[1,1024,1536]{1,2,0:T(8,128)(2,1)}) fusion(bf16[1,1024,3072]{1,2,0:T(8,128)(2,1)} %constant_dynamic-update-slice_fusion.2), kind=kLoop, calls=%fused_computation.190 | loop fusion | bytes 12582912 | tf_op jit(solution)/shard_map/slice | solution.py:155
  414.2 3.9 fusion.7
  418.1 3.0 fusion.11
  421.2 4.7 fusion.79
  425.9 4.9 fusion.135
  430.9 4.4 collective-permute-start.1
  435.3 0.3 fusion.120
  435.6 8.8 %copy.56 = bf16[1,1024,3072]{1,2,0:T(8,128)(2,1)} copy(bf16[1,1024,3072]{2,1,0:T(8,128)(2,1)} %get-tuple-element.32) | data formatting | bytes 12582912
  444.5 3.9 copy.72
  448.4 3.2 collective-permute-done.1
  451.8 0.4 multiply_reduce_fusion.3
  452.2 7.5 %fusion.21 = f32[1,256,4608]{2,1,0:T(8,128)S(1)} fusion(bf16[1,1536,4608]{2,1,0:T(8,128)(2,1)} %all-gather.6.cloned.1.call-done, f32[1536]{0:T(1024)S(1)} %get-tuple-element.21, f32[1536]{0:T(1024)S(1)} %get-tuple-element.16, f32[256]{0:T(256)S(1)} %add_rsqrt_fusion.3, f32[256]{0:T(256)S(1)} %broadcast_multiply_fusion.1, ...), kind=kOutput, calls=%fused_computation.23 | convolution fusion | flops 3626631168 | bytes 21252096 | tf_op jit(solution)/shard_map/dot_general | solution.py:107
  460.1 1.2 multiply_convert_fusion
  461.3 1.3 pad_maximum_fusion.2
  462.6 2.6 copy.37
  465.2 2.7 constant_dynamic-update-slice_fusion
  467.9 6.2 %fusion.132 = (bf16[1,1024,1536]{1,2,0:T(8,128)(2,1)}, bf16[1,1024,1536]{1,2,0:T(8,128)(2,1)}) fusion(bf16[1,1024,3072]{1,2,0:T(8,128)(2,1)} %constant_dynamic-update-slice_fusion), kind=kLoop, calls=%fused_computation.189 | loop fusion | bytes 12582912 | tf_op jit(solution)/shard_map/slice | solution.py:155
  474.1 2.3 copy.38
  476.4 4.2 fusion.8
  480.6 3.0 fusion.13
  483.6 4.7 fusion.78
  488.4 5.5 %fusion.72 = f32[2,256,1536]{2,1,0:T(8,128)} fusion(f32[2,256,1536]{2,1,0:T(8,128)} %get-tuple-element.52, s32[]{:T(128)S(6)} %min.12, bf16[256,1536]{0,1:T(8,128)(2,1)S(1)} %bitcast.204, bf16[1,1536,1536]{2,1,0:T(8,128)(2,1)} %all-gather.8.cloned.1.call-done, f32[1536]{0:T(1024)S(1)} %get-tuple-element.15, pred[]{:T(512)S(6)} %select_n.179, ...), kind=kOutput, calls=%fused_computation.55 | convolution fusion | flops 1209925632 | bytes 11016198 | tf_op jit(solution)/shard_map/dot_general | solution.py:110
  493.9 2.2 reduce_sum.187
  496.0 2.5 multiply_reduce_fusion
  498.6 2.7 fusion.88
  501.3 1.3 collective-permute-start.2
  502.6 2.3 bitcast_dynamic-update-slice_fusion
  504.9 2.2 collective-permute-done.2
  507.1 0.6 fusion.113
  507.7 0.7 fusion.112
  (78 shorter events, 3.7 us)
Async XLA Ops:
  7.2 428.1 %copy-start = (f32[50,3072]{1,0:T(8,128)S(1)}, f32[50,3072]{1,0:T(8,128)}, u32[]{:S(2)}) copy-start(f32[50,3072]{1,0:T(8,128)} %param.19) | copy-start | bytes 1843204
  7.2 223.4 %all-gather.4.cloned.1.call-start = ((), (), s32[]{:S(2)}) async-start(), calls=%async_computation | async-start | bytes 15728640 | tf_op jit(solution)/shard_map/all_gather | solution.py:131
  7.9 1.5 copy-start.11
  7.9 7.2 %copy-start.12 = (bf16[64,1536]{1,0:T(8,128)(2,1)S(1)}, bf16[64,1536]{1,0:T(8,128)(2,1)}, u32[]{:S(2)}) copy-start(bf16[64,1536]{1,0:T(8,128)(2,1)} %param.14) | copy-start | bytes 589828
  7.9 313.5 %all-gather.6.cloned.1.call-start = ((), (), s32[]{:S(2)}) async-start(), calls=%async_computation.1 | async-start | bytes 17694720 | tf_op jit(solution)/shard_map/all_gather | solution.py:100
  8.7 351.8 %all-gather.8.cloned.1.call-start = ((), (), s32[]{:S(2)}) async-start(), calls=%async_computation.2 | async-start | bytes 5898240 | tf_op jit(solution)/shard_map/all_gather | solution.py:101
  15.1 2.6 copy-start.13
  15.1 2.7 copy-start.14
  15.1 3.0 copy-start.10
  15.1 3.0 copy-start.15
  15.7 1.6 copy-start.1
  360.5 3.0 copy-start.2
  368.4 20.6 %collective-permute-start = (bf16[1,256,1536]{2,1,0:T(8,128)(2,1)S(1)}, bf16[1,256,1536]{2,1,0:T(8,128)(2,1)S(1)}, u32[]{:S(2)}, u32[]{:S(2)}) collective-permute-start(bf16[1,256,1536]{2,1,0:T(8,128)(2,1)S(1)} %bitcast.213), channel_id=1, source_target_pairs={{0,16},{1,17},{2,18},{3,19},{4,20},{5,21},{6,22},{7,23},{8,24},{9,... | collective-permute-start | bytes 2359304 | tf_op jit(solution)/shard_map/ppermute | solution.py:16
  380.6 11.8 %copy-start.3 = (f32[512,1536]{1,0:T(8,128)S(1)}, f32[512,1536]{1,0:T(8,128)}, u32[]{:S(2)}) copy-start(f32[512,1536]{1,0:T(8,128)} %copy-done.1) | copy-start | bytes 9437188
  407.6 6.3 %copy-start.9 = (bf16[1,256,1536]{2,1,0:T(8,128)(2,1)S(1)}, bf16[1,256,1536]{2,1,0:T(8,128)(2,1)}, u32[]{:S(2)}) copy-start(bf16[1,256,1536]{2,1,0:T(8,128)(2,1)} %get-tuple-element.43) | copy-start | bytes 2359300
  421.2 4.8 copy-start.4
  430.9 20.7 %collective-permute-start.1 = (bf16[1,256,1536]{2,1,0:T(8,128)(2,1)S(1)}, bf16[1,256,1536]{2,1,0:T(8,128)(2,1)S(1)}, u32[]{:S(2)}, u32[]{:S(2)}) collective-permute-start(bf16[1,256,1536]{2,1,0:T(8,128)(2,1)S(1)} %get-tuple-element.51), channel_id=1, source_target_pairs={{0,16},{1,17},{2,18},{3,19},{4,20},{5,21},{6,22},{7,23},{8,24},{9,... | collective-permute-start | bytes 2359304 | tf_op jit(solution)/shard_map/ppermute | solution.py:16
  444.5 7.1 %copy-start.5 = (f32[512,1536]{1,0:T(8,128)S(1)}, f32[512,1536]{1,0:T(8,128)}, u32[]{:S(2)}) copy-start(f32[512,1536]{1,0:T(8,128)} %copy-done.1) | copy-start | bytes 9437188
  483.6 4.8 copy-start.6
  493.9 4.7 copy-start.16
  496.0 6.5 %copy-start.7 = (bf16[1,2,1,256,3072]{4,3,1,2,0:T(8,128)(2,1)S(1)}, bf16[1,2,1,256,3072]{4,3,1,2,0:T(8,128)(2,1)}, u32[]{:S(2)}) copy-start(bf16[1,2,1,256,3072]{4,3,1,2,0:T(8,128)(2,1)} %copy.72) | copy-start | bytes 9437188
  501.3 5.8 %collective-permute-start.2 = (bf16[2,128,64]{1,2,0:T(8,128)(2,1)S(1)}, bf16[2,128,64]{1,2,0:T(8,128)(2,1)S(1)}, u32[]{:S(2)}, u32[]{:S(2)}) collective-permute-start(bf16[2,128,64]{1,2,0:T(8,128)(2,1)S(1)} %slice.225), channel_id=1, source_target_pairs={{16,0},{17,1},{18,2},{19,3},{20,4},{21,5},{22,6},{23,7},{24,8},{25... | collective-permute-start | bytes 98312 | tf_op jit(solution)/shard_map/ppermute | solution.py:16
  504.9 3.5 copy-start.8
Sparse Core Ops, SparseCore 0:
  9.6 220.9 all-gather.3
  232.1 89.2 all-gather.5
  323.0 37.4 all-gather.7
where the time goes:
time: 526 us; the launch traced here: 515 us
  waiting for transfers between devices  304 us (58%)
  local copies, waits for them, and re-layouts  86.1 us (16%)
  matrix products  65.1 us (12%)
  other arithmetic  30.9 us (6%)
  between operations  14.6 us (3%)
  starting transfers between devices  9.2 us (2%)
  blocking collectives  5.51 us (1%)
    all_gather x1, waiting for transfers between devices, body(): lax.all_gather(stale_cache, 'patch', axis=2, tiled=True)[0]  212 us
    all_gather x1, waiting for transfers between devices, body(): lax.all_gather(wqkv, 'fsdp', axis=1, tiled=True)  66.1 us
    unnamed x43, local copies, waits for them, and re-layouts  32.8 us
    dot_general x3, matrix products, project_in(): return jnp.dot(left, proj_full, preferred_element_type=jnp.float32)  22.8 us
    slice x3, local copies, waits for them, and re-layouts, attend_fn(): seen_rows[..., :model_width]  16 us
    dynamic_slice x1, local copies, waits for them, and re-layouts, body(): lax.dynamic_slice_in_dim(stale_all, first_video, group_size, 0)  16 us
    dot_general x3, matrix products, project_out(): return jnp.dot(left, out_full, preferred_element_type=jnp.float32)  15.3 us
    ppermute x3, waiting for transfers between devices, shifted(): return lax.ppermute(shard, axis, pairs)  13.7 us
  transfers between devices with their start and end apart: 6, of which 6 were waited for; matrix products, arithmetic and copies ran while one was open for 16% of the time, Pallas kernels for 0%

commit v1 on v0

--- a/solution.py
+++ b/solution.py
@@ -8,6 +8,28 @@
 HD = 128
 TSTEPS = 50
 EPS = 1e-06
+
+
+def in_order(blocks, dim):
+    shape = list(blocks.shape[1:])
+    shape[dim] *= blocks.shape[0]
+    return jnp.moveaxis(blocks, 0, dim).reshape(shape)
+
+
+def gather_around(shard, axis, dim):
+    peers = lax.axis_size(axis)
+    pairs = [(i, (i + 1) % peers) for i in range(peers)]
+    back = [(b, a) for a, b in pairs]
+    lower, upper = ([], [])
+    for lap in range(peers - 1):
+        if lap % 2 == 0:
+            lower.append(lax.ppermute(lower[-1] if lower else shard, axis, pairs))
+        else:
+            upper.append(lax.ppermute(upper[-1] if upper else shard, axis, back))
+    parts = jnp.stack([*lower[::-1], shard, *upper])
+    shift = lax.axis_index(axis) - len(lower)
+    parts = parts[(jnp.arange(peers) - shift) % peers]
+    return in_order(parts, dim)
 
 
 def shifted(shard, axis, by):
@@ -97,7 +119,7 @@
     patch_count = counts.shape[1]
     zero_index = jnp.zeros((), jnp.int32)
     proj_full, out_full = (
-        lax.all_gather(wqkv, "fsdp", axis=1, tiled=True),
+        gather_around(wqkv, "fsdp", 1),
         lax.all_gather(wo, "fsdp", axis=1, tiled=True),
     )
     proj_full = proj_full[0]

time: 526 us -> 427 us (0.81); the launches traced: 515 us -> 423 us
  waiting for transfers between devices: 304 us -> 175 us
  local copies, waits for them, and re-layouts: 86.1 us -> 105 us
  other arithmetic: 30.9 us -> 47.7 us
    all_gather x1, waiting for transfers between devices: 212 us -> 56.1 us  [body(): lax.all_gather(stale_cache, 'patch', axis=2, tiled=True)[0]]
    ppermute x0 -> x3, waiting for transfers between devices: none -> 103 us  [the longest x2 103 us: gather_around(): lower.append(lax.ppermute(lower[-1] if lower else shard, axis, pairs))]
    all_gather x1 -> x0, waiting for transfers between devices: 66.1 us -> none  [body(): lax.all_gather(wqkv, 'fsdp', axis=1, tiled=True)]
    gather x0 -> x3, local copies, waits for them, and re-layouts: none -> 19.2 us  [gather_around(): parts = parts[(jnp.arange(peers) - shift) % peers]]
    all_gather x1, waiting for transfers between devices: 10.2 us -> 0.85 us  [body(): lax.all_gather(wo, 'fsdp', axis=1, tiled=True)]
    unnamed x2 -> x3, other arithmetic: 1.34 us -> 8.8 us
    another operation x0 -> x1, other arithmetic: none -> 7.33 us  [gather_around(): parts = jnp.stack([*lower[::-1], shard, *upper])]
    unnamed x43 -> x61, local copies, waits for them, and re-layouts: 32.8 us -> 33.7 us
  transfers between devices with their start and end apart: 6 -> 8, of which waited for: 6 -> 7; matrix products, arithmetic and copies ran while one was open for 16% -> 26% of each run, Pallas kernels for 0% -> 0%
where the time goes in v1:
time: 427 us; the launch traced here: 423 us
  waiting for transfers between devices  175 us (41%)
  local copies, waits for them, and re-layouts  105 us (25%)
  matrix products  61.4 us (14%)
  other arithmetic  47.7 us (11%)
  between operations  14.9 us (3%)
  starting transfers between devices  14.3 us (3%)
  blocking collectives  4.61 us (1%)
    ppermute x2, waiting for transfers between devices, gather_around(): lower.append(lax.ppermute(lower[-1] if lower else shard, axis, pairs))  103 us
    all_gather x1, waiting for transfers between devices, body(): lax.all_gather(stale_cache, 'patch', axis=2, tiled=True)[0]  56.1 us
    unnamed x61, local copies, waits for them, and re-layouts  33.7 us
    gather x3, local copies, waits for them, and re-layouts, gather_around(): parts = parts[(jnp.arange(peers) - shift) % peers]  19.2 us
    dot_general x3, matrix products, project_in(): return jnp.dot(left, proj_full, preferred_element_type=jnp.float32)  18.9 us
    slice x3, local copies, waits for them, and re-layouts, attend_fn(): seen_rows[..., :model_width]  16 us
    dot_general x3, matrix products, project_out(): return jnp.dot(left, out_full, preferred_element_type=jnp.float32)  15.3 us
    dynamic_slice x1, local copies, waits for them, and re-layouts, body(): lax.dynamic_slice_in_dim(stale_all, first_video, group_size, 0)  14.4 us
  transfers between devices with their start and end apart: 8, of which 7 were waited for; matrix products, arithmetic and copies ran while one was open for 26% of the time, Pallas kernels for 0%

profile of v1, /device:TPU:0, one launch (start us, length us, event | category | flops | bytes accessed | tf_op | source)
XLA Modules:
  0.0 422.9 jit_solution(16945101103817618173)
XLA Ops:
  8.5 2.0 collective-permute-start.2
  10.6 74.7 %collective-permute-done = bf16[1,384,4608]{2,1,0:T(8,128)(2,1)} collective-permute-done((bf16[1,384,4608]{2,1,0:T(8,128)(2,1)}, bf16[1,384,4608]{2,1,0:T(8,128)(2,1)}, u32[]{:S(2)}, u32[]{:S(2)}) %collective-permute-start) | collective-permute-done | bytes 3538976 | tf_op jit(solution)/shard_map/ppermute | solution.py:26
  85.2 2.5 collective-permute-start.1
  87.8 4.6 %all_gather.9 = bf16[2,1,256,64]{2,3,1,0:T(8,128)(2,1)S(1)} all-gather(bf16[2,1,128,64]{2,3,1,0:T(8,128)(2,1)S(1)} %convert_element_type.99), channel_id=1, replica_groups=mesh['section'=2,'patch'=4,'fsdp'=4] {'section'}, dimensions={2}, use_global_device_ids=true | all-gather | bytes 98304 | tf_op jit(solution)/shard_map/all_gather | solution.py:134
  96.2 1.4 copy-done.1
  97.9 28.5 %collective-permute-done.1 = bf16[1,384,4608]{2,1,0:T(8,128)(2,1)} collective-permute-done((bf16[1,384,4608]{2,1,0:T(8,128)(2,1)}, bf16[1,384,4608]{2,1,0:T(8,128)(2,1)}, u32[]{:S(2)}, u32[]{:S(2)}) %collective-permute-start.1) | collective-permute-done | bytes 3538976 | tf_op jit(solution)/shard_map/ppermute | solution.py:26
  126.5 7.3 %pad_maximum_fusion = bf16[4,1,384,4608]{3,2,1,0:T(8,128)(2,1)S(1)} fusion(bf16[1,1,384,4608]{3,2,1,0:T(8,128)(2,1)} %bitcast.4, bf16[1,1,384,4608]{3,2,1,0:T(8,128)(2,1)S(1)} %bitcast.205, bf16[1,1,384,4608]{3,2,1,0:T(8,128)(2,1)} %bitcast.2, bf16[1,1,384,4608]{3,2,1,0:T(8,128)(2,1)} %bitcast.1), kind=kLoop, calls=%fused_computation.2 | loop fusion | flops 21233664 | bytes 28311552 | tf_op jit(solution)/shard_map/stack | solution.py:29
  133.8 5.3 %slice_bitcast_fusion.1 = (bf16[4,384,2304]{2,1,0:T(8,128)(2,1)}, bf16[4,384,2304]{2,1,0:T(8,128)(2,1)}) fusion(bf16[4,1,384,4608]{3,2,1,0:T(8,128)(2,1)S(1)} %pad_maximum_fusion), kind=kLoop, calls=%fused_computation.20 | loop fusion | bytes 28311552 | tf_op jit(solution)/shard_map/gather | solution.py:31
  139.1 7.0 %gather_fusion = bf16[4,384,2304]{2,1,0:T(8,128)(2,1)} fusion(bf16[4,384,2304]{2,1,0:T(8,128)(2,1)} %get-tuple-element.32, s32[1024]{0:T(1024)S(1)} %pad_clamp_fusion), kind=kCustom, calls=%fused_computation | custom fusion | bytes 14155792 | tf_op jit(solution)/shard_map/gather | solution.py:31
  146.1 6.9 %gather_fusion.1 = bf16[4,384,2304]{2,1,0:T(8,128)(2,1)} fusion(bf16[4,384,2304]{2,1,0:T(8,128)(2,1)} %get-tuple-element.33, s32[1024]{0:T(1024)S(1)} %pad_clamp_fusion), kind=kCustom, calls=%fused_computation.1 | custom fusion | bytes 14155792 | tf_op jit(solution)/shard_map/gather | solution.py:31
  153.0 7.5 %pad_maximum_fusion.1 = bf16[4,1,384,4608]{3,2,0,1:T(8,128)(2,1)S(1)} fusion(bf16[4,1,384,2304]{3,2,0,1:T(8,128)(2,1)} %bitcast.197, bf16[4,1,384,2304]{3,2,0,1:T(8,128)(2,1)} %bitcast.196), kind=kLoop, calls=%fused_computation.3 | loop fusion | flops 28311552 | bytes 28311552
  160.5 3.9 convolution_bitcast_fusion.2
  164.5 1.1 copy-done.8
  165.9 1.2 multiply_convert_fusion.4
  167.1 2.0 broadcast_in_dim.156
  169.1 2.3 select_dynamic-update-slice_fusion.1
  171.4 1.7 copy.29
  173.1 1.4 copy.30
  174.5 56.1 %all-gather.3.cloned.1.call-done = bf16[1,2,4,256,3072]{4,3,2,1,0:T(8,128)(2,1)} async-done(((bf16[1,2,1,256,3072]{4,3,2,1,0:T(8,128)(2,1)}), bf16[1,2,4,256,3072]{4,3,2,1,0:T(8,128)(2,1)}) %all-gather.3.cloned.1.call-update) | async-done | bytes 12582928 | tf_op jit(solution)/shard_map/all_gather | solution.py:153
  230.6 14.4 %constant_dynamic-slice_fusion.3 = (bf16[1,1024,3072]{2,1,0:T(8,128)(2,1)}, bf16[1,1024,3072]{2,1,0:T(8,128)(2,1)}, bf16[1,1024,3072]{2,1,0:T(8,128)(2,1)}) fusion(bf16[2,1024,3072]{2,1,0:T(8,128)(2,1)} %bitcast.198, s32[]{:T(128)S(6)} %min.12, s32[]{:T(128)S(6)} %min.11, s32[]{:T(128)S(6)} %min.10), kind=kLoop, calls=%fused_computation.146 | loop fusion | bytes 37748748 | tf_op jit(solution)/shard_map/dynamic_slice | solution.py:169
  245.0 8.6 %copy.54 = bf16[1,1024,3072]{1,2,0:T(8,128)(2,1)} copy(bf16[1,1024,3072]{2,1,0:T(8,128)(2,1)} %get-tuple-element.36) | data formatting | bytes 12582912
  253.6 1.3 constant_dynamic-update-slice_fusion.3
  254.9 3.6 fusion.121
  258.4 2.0 fusion
  260.5 3.0 fusion.3
  263.5 3.4 fusion.65
  267.8 2.0 broadcast_in_dim.85
  270.9 4.9 %bitcast_dynamic-update-slice_fusion.1 = (f32[2,256,1536]{2,1,0:T(8,128)}, bf16[256,1536]{1,0:T(8,128)(2,1)S(1)}) fusion(f32[2,256,1536]{2,1,0:T(8,128)} %broadcast_in_dim.85, s32[]{:T(128)S(6)} %min.10, pred[]{:T(512)S(6)} %eq.29, bf16[256,1536]{0,1:T(8,128)(2,1)S(1)} %bitcast.223, bf16[1,1536,1536]{2,1,0:T(8,128)(2,1)} %all-gather.5.cloned.1.call-done, ...), kind=kOutput, calls=%fused_computation.72 | convolution fusion | flops 1209925632 | bytes 9443333 | tf_op jit(solution)/shard_map/dot_general | solution.py:132
  275.8 3.4 collective-permute-start.3
  279.2 8.6 %copy.55 = bf16[1,1024,3072]{1,2,0:T(8,128)(2,1)} copy(bf16[1,1024,3072]{2,1,0:T(8,128)(2,1)} %get-tuple-element.35) | data formatting | bytes 12582912
  287.8 8.5 %collective-permute-done.3 = bf16[1,256,1536]{2,1,0:T(8,128)(2,1)S(1)} collective-permute-done((bf16[1,256,1536]{2,1,0:T(8,128)(2,1)S(1)}, bf16[1,256,1536]{2,1,0:T(8,128)(2,1)S(1)}, u32[]{:S(2)}, u32[]{:S(2)}) %collective-permute-start.3) | collective-permute-done | bytes 786464 | tf_op jit(solution)/shard_map/ppermute | solution.py:38
  296.4 1.6 fusion.117
  298.0 1.8 multiply_reduce_fusion.6
  299.8 7.5 %convolution_bitcast_fusion.1 = f32[1,256,4608]{2,1,0:T(8,128)S(1)} fusion(bf16[1536,4608]{1,0:T(8,128)(2,1)} %bitcast.200, f32[1536]{0:T(1024)S(1)} %get-tuple-element.22, f32[1536]{0:T(1024)S(1)} %get-tuple-element.17, f32[256]{0:T(256)S(1)} %add_rsqrt_fusion.6, f32[256]{0:T(256)S(1)} %broadcast_multiply_fusion.2, ...), kind=kOutput, calls=%fused_computation.22 | convolution fusion | flops 3626631168 | bytes 21252096 | tf_op jit(solution)/shard_map/dot_general | solution.py:129
  307.7 1.2 multiply_convert_fusion.2
  308.9 1.7 select_dynamic-update-slice_fusion
  310.6 1.6 copy.33
  312.2 2.7 constant_dynamic-update-slice_fusion.2
  314.9 6.3 %fusion.120 = (bf16[1,1024,1536]{1,2,0:T(8,128)(2,1)}, bf16[1,1024,1536]{1,2,0:T(8,128)(2,1)}) fusion(bf16[1,1024,3072]{1,2,0:T(8,128)(2,1)} %constant_dynamic-update-slice_fusion.2), kind=kLoop, calls=%fused_computation.197 | loop fusion | bytes 12582912 | tf_op jit(solution)/shard_map/slice | solution.py:177
  321.4 3.9 fusion.1
  325.4 3.0 fusion.5
  328.4 4.7 %fusion.64 = bf16[1,256,12,128]{1,3,2,0:T(8,128)(2,1)S(1)} fusion(bf16[1024,12,128]{0,2,1:T(8,128)(2,1)} %bitcast.211, f32[12,256,1024]{2,1,0:T(8,128)S(1)} %get-tuple-element.60, f32[12,256]{1,0:T(8,128)S(1)} %get-tuple-element.59, pred[1024]{0:T(1024)(128)(4,1)S(1)} %get-tuple-element.27, f32[256,12]{0,1:T(8,128)S(1)} %bitcast.219), kind=kOutput, calls=%fused_computation.69 | convolution fusion | flops 818675712 | bytes 16540672 | tf_op jit(solution)/shard_map/ghqk,gkhd->gqhd/dot_general | solution.py:71
  333.2 4.9 %fusion.122 = (bf16[1,256,1536]{2,1,0:T(8,128)(2,1)S(1)}, f32[2,256,1536]{2,1,0:T(8,128)}) fusion(f32[2,256,1536]{2,1,0:T(8,128)} %get-tuple-element.61, s32[]{:T(128)S(6)} %min.11, bf16[256,1536]{0,1:T(8,128)(2,1)S(1)} %bitcast.214, bf16[1,1536,1536]{2,1,0:T(8,128)(2,1)} %all-gather.5.cloned.1.call-done, f32[1536]{0:T(1024)S(1)} %get-tuple-element.18, ...), kind=kOutput, calls=%fused_computation.199 | convolution fusion | flops 1209925632 | bytes 10229765 | tf_op jit(solution)/shard_map/dot_general | solution.py:132
  338.1 4.5 %collective-permute-start.4 = (bf16[1,256,1536]{2,1,0:T(8,128)(2,1)S(1)}, bf16[1,256,1536]{2,1,0:T(8,128)(2,1)S(1)}, u32[]{:S(2)}, u32[]{:S(2)}) collective-permute-start(bf16[1,256,1536]{2,1,0:T(8,128)(2,1)S(1)} %get-tuple-element.53), channel_id=1, source_target_pairs={{0,16},{1,17},{2,18},{3,19},{4,20},{5,21},{6,22},{7,23},{8,24},{9,... | collective-permute-start | bytes 2359304 | tf_op jit(solution)/shard_map/ppermute | solution.py:38
  343.0 8.8 %copy.56 = bf16[1,1024,3072]{1,2,0:T(8,128)(2,1)} copy(bf16[1,1024,3072]{2,1,0:T(8,128)(2,1)} %get-tuple-element.34) | data formatting | bytes 12582912
  351.9 3.9 copy.72
  355.8 3.2 collective-permute-done.4
  359.6 7.5 %convolution_bitcast_fusion = f32[1,256,4608]{2,1,0:T(8,128)S(1)} fusion(bf16[1536,4608]{1,0:T(8,128)(2,1)} %bitcast.201, f32[1536]{0:T(1024)S(1)} %get-tuple-element.21, f32[1536]{0:T(1024)S(1)} %get-tuple-element.16, f32[256]{0:T(256)S(1)} %add_rsqrt_fusion.3, f32[256]{0:T(256)S(1)} %broadcast_multiply_fusion.1, ...), kind=kOutput, calls=%fused_computation.21 | convolution fusion | flops 3626631168 | bytes 21252096 | tf_op jit(solution)/shard_map/dot_general | solution.py:129
  367.5 1.2 multiply_convert_fusion
  368.7 1.4 pad_maximum_fusion.4
  370.0 2.6 copy.37
  372.6 2.7 constant_dynamic-update-slice_fusion
  375.3 6.2 %fusion.119 = (bf16[1,1024,1536]{1,2,0:T(8,128)(2,1)}, bf16[1,1024,1536]{1,2,0:T(8,128)(2,1)}) fusion(bf16[1,1024,3072]{1,2,0:T(8,128)(2,1)} %constant_dynamic-update-slice_fusion), kind=kLoop, calls=%fused_computation.196 | loop fusion | bytes 12582912 | tf_op jit(solution)/shard_map/slice | solution.py:177
  381.5 2.3 copy.38
  383.8 4.2 fusion.2
  388.0 3.0 fusion.7
  391.0 4.7 %fusion.63 = bf16[1,256,12,128]{1,3,2,0:T(8,128)(2,1)S(1)} fusion(bf16[1024,12,128]{0,2,1:T(8,128)(2,1)} %bitcast.210, f32[12,256,1024]{2,1,0:T(8,128)S(1)} %get-tuple-element.64, f32[12,256]{1,0:T(8,128)S(1)} %get-tuple-element.63, pred[1024]{0:T(1024)(128)(4,1)S(1)} %copy-done.19, f32[256,12]{0,1:T(8,128)S(1)} %bitcast.220), kind=kOutput, calls=%fused_computation.67 | convolution fusion | flops 818675712 | bytes 16540672 | tf_op jit(solution)/shard_map/ghqk,gkhd->gqhd/dot_general | solution.py:71
  395.8 5.5 %fusion.57 = f32[2,256,1536]{2,1,0:T(8,128)} fusion(f32[2,256,1536]{2,1,0:T(8,128)} %get-tuple-element.54, s32[]{:T(128)S(6)} %min.12, bf16[256,1536]{0,1:T(8,128)(2,1)S(1)} %bitcast.213, bf16[1,1536,1536]{2,1,0:T(8,128)(2,1)} %all-gather.5.cloned.1.call-done, f32[1536]{0:T(1024)S(1)} %copy-done.17, pred[]{:T(512)S(6)} %select_n.205, ...), kind=kOutput, calls=%fused_computation.55 | convolution fusion | flops 1209925632 | bytes 11016198 | tf_op jit(solution)/shard_map/dot_general | solution.py:132
  401.3 2.2 reduce_sum.187
  403.5 2.5 multiply_reduce_fusion
  406.0 2.7 fusion.73
  408.7 1.3 collective-permute-start.5
  410.0 2.3 bitcast_dynamic-update-slice_fusion
  412.3 2.2 collective-permute-done.5
  (106 shorter events, 11.0 us)
Async XLA Ops:
  7.2 335.5 %copy-start = (f32[50,3072]{1,0:T(8,128)S(1)}, f32[50,3072]{1,0:T(8,128)}, u32[]{:S(2)}) copy-start(f32[50,3072]{1,0:T(8,128)} %param.19) | copy-start | bytes 1843204
  7.2 80.6 %copy-start.14 = (f32[2,1,128,64]{2,3,1,0:T(8,128)S(1)}, f32[2,1,128,64]{2,3,1,0:T(8,128)}, u32[]{:S(2)}) copy-start(f32[2,1,128,64]{2,3,1,0:T(8,128)} %param.11) | copy-start | bytes 196612
  7.2 85.3 %copy-start.22 = (s32[2,4]{1,0:T(2,128)S(1)}, s32[2,4]{1,0:T(2,128)}, u32[]{:S(2)}) copy-start(s32[2,4]{1,0:T(2,128)} %param.12) | copy-start | bytes 100
  7.2 86.8 %copy-start.23 = (s32[2]{0:T(128)S(1)}, s32[2]{0:T(128)}, u32[]{:S(2)}) copy-start(s32[2]{0:T(128)} %param.13) | copy-start | bytes 28
  7.2 86.8 %copy-start.13 = (f32[1,50,4608]{2,0,1:T(1,128)S(1)}, f32[1,50,4608]{2,0,1:T(1,128)}, u32[]{:S(2)}) copy-start(f32[1,50,4608]{2,0,1:T(1,128)} %param.18) | copy-start | bytes 2764804
  7.2 88.1 %copy-start.18 = (f32[1,3072]{1,0:T(1,128)S(1)}, f32[1,3072]{1,0:T(1,128)}, u32[]{:S(2)}) copy-start(f32[1,3072]{1,0:T(1,128)} %param.17) | copy-start | bytes 36868
  7.2 88.1 %copy-start.16 = (bf16[64,1536]{1,0:T(8,128)(2,1)S(1)}, bf16[64,1536]{1,0:T(8,128)(2,1)}, u32[]{:S(2)}) copy-start(bf16[64,1536]{1,0:T(8,128)(2,1)} %param.14) | copy-start | bytes 589828
  7.2 223.3 %all-gather.3.cloned.1.call-start = ((), (), s32[]{:S(2)}) async-start(), calls=%async_computation | async-start | bytes 15728640 | tf_op jit(solution)/shard_map/all_gather | solution.py:153
  8.0 259.9 %all-gather.5.cloned.1.call-start = ((), (), s32[]{:S(2)}) async-start(), calls=%async_computation.1 | async-start | bytes 5898240 | tf_op jit(solution)/shard_map/all_gather | solution.py:123
  8.0 77.2 %collective-permute-start = (bf16[1,384,4608]{2,1,0:T(8,128)(2,1)}, bf16[1,384,4608]{2,1,0:T(8,128)(2,1)}, u32[]{:S(2)}, u32[]{:S(2)}) collective-permute-start(bf16[1,384,4608]{2,1,0:T(8,128)(2,1)} %param.15), channel_id=1, source_target_pairs={{0,1},{1,2},{2,3},{3,0},{4,5},{5,6},{6,7},{7,4},{8,9},{9,10},{10,1... | collective-permute-start | bytes 10616840 | tf_op jit(solution)/shard_map/ppermute | solution.py:26
  8.5 89.4 %collective-permute-start.2 = (bf16[1,384,4608]{2,1,0:T(8,128)(2,1)}, bf16[1,384,4608]{2,1,0:T(8,128)(2,1)}, u32[]{:S(2)}, u32[]{:S(2)}) collective-permute-start(bf16[1,384,4608]{2,1,0:T(8,128)(2,1)} %param.15), channel_id=1, source_target_pairs={{1,0},{2,1},{3,2},{0,3},{5,4},{6,5},{7,6},{4,7},{9,8},{10,9},{11,1... | collective-permute-start | bytes 10616840 | tf_op jit(solution)/shard_map/ppermute | solution.py:28
  85.2 41.2 %collective-permute-start.1 = (bf16[1,384,4608]{2,1,0:T(8,128)(2,1)}, bf16[1,384,4608]{2,1,0:T(8,128)(2,1)}, u32[]{:S(2)}, u32[]{:S(2)}) collective-permute-start(bf16[1,384,4608]{2,1,0:T(8,128)(2,1)} %collective-permute-done), channel_id=1, source_target_pairs={{0,1},{1,2},{2,3},{3,0},{4,5},{5,6},{6,7},{7,4},{8,9},{9,10},{10,1... | collective-permute-start | bytes 10616840 | tf_op jit(solution)/shard_map/ppermute | solution.py:26
  92.8 0.6 copy-start.20
  95.3 31.1 %copy-start.9 = (bf16[1,384,4608]{2,1,0:T(8,128)(2,1)S(1)}, bf16[1,384,4608]{2,1,0:T(8,128)(2,1)}, u32[]{:S(2)}) copy-start(bf16[1,384,4608]{2,1,0:T(8,128)(2,1)} %param.15) | copy-start | bytes 10616836
  95.9 1.6 copy-start.1
  153.0 7.5 %copy-start.2 = (f32[512,1536]{1,0:T(8,128)S(1)}, f32[512,1536]{1,0:T(8,128)}, u32[]{:S(2)}) copy-start(f32[512,1536]{1,0:T(8,128)} %copy-done.1) | copy-start | bytes 9437188
  160.5 5.1 %copy-start.8 = (bf16[4,1,384,4608]{3,2,0,1:T(8,128)(2,1)}, bf16[4,1,384,4608]{3,2,0,1:T(8,128)(2,1)S(1)}, u32[]{:S(2)}) copy-start(bf16[4,1,384,4608]{3,2,0,1:T(8,128)(2,1)S(1)} %pad_maximum_fusion.1) | copy-start | bytes 42467332
  267.8 3.0 copy-start.3
  275.8 20.6 %collective-permute-start.3 = (bf16[1,256,1536]{2,1,0:T(8,128)(2,1)S(1)}, bf16[1,256,1536]{2,1,0:T(8,128)(2,1)S(1)}, u32[]{:S(2)}, u32[]{:S(2)}) collective-permute-start(bf16[1,256,1536]{2,1,0:T(8,128)(2,1)S(1)} %bitcast.222), channel_id=1, source_target_pairs={{0,16},{1,17},{2,18},{3,19},{4,20},{5,21},{6,22},{7,23},{8,24},{9,... | collective-permute-start | bytes 2359304 | tf_op jit(solution)/shard_map/ppermute | solution.py:38
  287.8 11.9 %copy-start.4 = (f32[512,1536]{1,0:T(8,128)S(1)}, f32[512,1536]{1,0:T(8,128)}, u32[]{:S(2)}) copy-start(f32[512,1536]{1,0:T(8,128)} %copy-done.1) | copy-start | bytes 9437188
  314.9 6.3 %copy-start.12 = (bf16[1,256,1536]{2,1,0:T(8,128)(2,1)S(1)}, bf16[1,256,1536]{2,1,0:T(8,128)(2,1)}, u32[]{:S(2)}) copy-start(bf16[1,256,1536]{2,1,0:T(8,128)(2,1)} %get-tuple-element.45) | copy-start | bytes 2359300
  328.4 4.8 %copy-start.5 = (f32[512,1536]{1,0:T(8,128)S(1)}, f32[512,1536]{1,0:T(8,128)}, u32[]{:S(2)}) copy-start(f32[512,1536]{1,0:T(8,128)} %copy-done.1) | copy-start | bytes 9437188
  338.1 20.8 %collective-permute-start.4 = (bf16[1,256,1536]{2,1,0:T(8,128)(2,1)S(1)}, bf16[1,256,1536]{2,1,0:T(8,128)(2,1)S(1)}, u32[]{:S(2)}, u32[]{:S(2)}) collective-permute-start(bf16[1,256,1536]{2,1,0:T(8,128)(2,1)S(1)} %get-tuple-element.53), channel_id=1, source_target_pairs={{0,16},{1,17},{2,18},{3,19},{4,20},{5,21},{6,22},{7,23},{8,24},{9,... | collective-permute-start | bytes 2359304 | tf_op jit(solution)/shard_map/ppermute | solution.py:38
  351.9 7.1 %copy-start.6 = (f32[512,1536]{1,0:T(8,128)S(1)}, f32[512,1536]{1,0:T(8,128)}, u32[]{:S(2)}) copy-start(f32[512,1536]{1,0:T(8,128)} %copy-done.1) | copy-start | bytes 9437188
  375.3 8.5 %copy-start.19 = (pred[1024]{0:T(1024)(128)(4,1)S(1)}, pred[1024]{0:T(1024)(128)(4,1)}, u32[]{:S(2)}) copy-start(pred[1024]{0:T(1024)(128)(4,1)} %get-tuple-element.26) | copy-start | bytes 3076
  391.0 4.8 %copy-start.7 = (f32[512,1536]{1,0:T(8,128)S(1)}, f32[512,1536]{1,0:T(8,128)}, u32[]{:S(2)}) copy-start(f32[512,1536]{1,0:T(8,128)} %copy-done.1) | copy-start | bytes 9437188
  391.0 4.8 %copy-start.17 = (f32[1536]{0:T(1024)S(1)}, f32[1536]{0:T(1024)}, u32[]{:S(2)}) copy-start(f32[1536]{0:T(1024)} %get-tuple-element.15) | copy-start | bytes 18436
  401.3 4.7 %copy-start.21 = (pred[2,256]{1,0:T(4,128)(4,1)S(1)}, pred[2,256]{1,0:T(4,128)(4,1)}, u32[]{:S(2)}) copy-start(pred[2,256]{1,0:T(4,128)(4,1)} %copy-done.20) | copy-start | bytes 1540
  401.3 4.7 %copy-start.25 = (bf16[1536,64]{0,1:T(8,128)(2,1)S(1)}, bf16[1536,64]{0,1:T(8,128)(2,1)}, u32[]{:S(2)}) copy-start(bf16[1536,64]{0,1:T(8,128)(2,1)} %param.20) | copy-start | bytes 589828
  403.4 6.5 %copy-start.10 = (bf16[1,2,1,256,3072]{4,3,1,2,0:T(8,128)(2,1)S(1)}, bf16[1,2,1,256,3072]{4,3,1,2,0:T(8,128)(2,1)}, u32[]{:S(2)}) copy-start(bf16[1,2,1,256,3072]{4,3,1,2,0:T(8,128)(2,1)} %copy.72) | copy-start | bytes 9437188
  403.5 6.5 %copy-start.24 = (pred[256]{0:T(512)(128)(4,1)S(1)}, pred[256]{0:T(512)(128)(4,1)}, u32[]{:S(2)}) copy-start(pred[256]{0:T(512)(128)(4,1)} %get-tuple-element.29) | copy-start | bytes 772
  408.7 6.5 %copy-start.15 = (f32[2,1,128,64]{2,3,1,0:T(8,128)S(1)}, f32[2,1,128,64]{2,3,1,0:T(8,128)}, u32[]{:S(2)}) copy-start(f32[2,1,128,64]{2,3,1,0:T(8,128)} %param.11) | copy-start | bytes 196612
  408.7 5.8 %collective-permute-start.5 = (bf16[2,128,64]{1,2,0:T(8,128)(2,1)S(1)}, bf16[2,128,64]{1,2,0:T(8,128)(2,1)S(1)}, u32[]{:S(2)}, u32[]{:S(2)}) collective-permute-start(bf16[2,128,64]{1,2,0:T(8,128)(2,1)S(1)} %slice.229), channel_id=1, source_target_pairs={{16,0},{17,1},{18,2},{19,3},{20,4},{21,5},{22,6},{23,7},{24,8},{25... | collective-permute-start | bytes 98312 | tf_op jit(solution)/shard_map/ppermute | solution.py:38
  412.3 3.5 copy-start.11
Sparse Core Ops, SparseCore 0:
  9.6 220.8 all-gather.2
  232.1 35.6 all-gather.4
